TPU v7x, 32 devices: a whole 2x2x4 slice. The times are simulated.
32 devices in a mesh: kv: 2 (over y), ctx: 16 (over z, x, core).
Axes of the slice: x: 2, y: 2, z: 4, core: 2. Of those that a mesh axis runs over, the one named last changes fastest.
Arguments:
- residual: bfloat16 [64, 8192], P(None, 'ctx'), may hold values from -8 to 8
- queries: bfloat16 [64, 8192], P(None, 'kv'), may hold values from -16 to 16
- draft_token_keys: bfloat16 [64, 1024], P(None, 'kv'), may hold values from -32 to 32
- draft_token_values: bfloat16 [64, 1024], P(None, 'kv'), may hold values from -8 to 8
- cache_keys: bfloat16 [2, 8192, 1024], P(None, 'ctx', 'kv'), may hold values from -32 to 32
- cached_value_rows: bfloat16 [2, 8192, 1024], P(None, 'ctx', 'kv'), may hold values from -8 to 8
- tenant_ids: int32 [64], replicated, may hold values from 0 to 1, as said below
- tree_mask: int32 [64, 64], replicated, may hold values from 0 to 1, as said below
- cache_lengths: int32 [2], replicated, may hold values from 4097 to 8192
- out_weight: bfloat16 [8192, 8192], P('kv', 'ctx'), may hold values from -0.0625 to 0.0625
- out_signs: bfloat16 [2, 8192, 8192], P(None, 'kv', 'ctx'), may hold values from -1 to 1, as said below
- norm_gain: float32 [8192], P('ctx'), may hold values from 0.1 to 1.9
- gate_weight: bfloat16 [8192, 16384], P(None, ('kv', 'ctx')), may hold values from -0.0625 to 0.0625
- up_weight: bfloat16 [8192, 16384], P(None, ('kv', 'ctx')), may hold values from -0.0625 to 0.0625
- down_weight: bfloat16 [16384, 8192], P(('kv', 'ctx')), may hold values from -0.09375 to 0.09375
- gate_signs: bfloat16 [2, 8192, 16384], P(None, None, ('kv', 'ctx')), may hold values from -1 to 1, as said below
- up_signs: bfloat16 [2, 8192, 16384], P(None, None, ('kv', 'ctx')), may hold values from -1 to 1, as said below
- down_signs: bfloat16 [2, 16384, 8192], P(None, ('kv', 'ctx')), may hold values from -1 to 1, as said below
- delta_scale: float32 [2, 4], replicated, may hold values from 0.3 to 0.9
Outputs:
- mixed: bfloat16 [64, 8192], P(None, 'ctx')
Inputs may be any that keep to these rules, and one draw needn't show every extreme that they name: `tenant_ids`: exactly 32 tokens belong to each tenant. `tree_mask`: entry (i, j) is 1 exactly when token j is token i or an ancestor of token i in the draft tree of their common tenant; each tenant's 32 tokens form one tree. `out_signs`: every entry is 1 or -1. `gate_signs`: every entry is 1 or -1. `up_signs`: every entry is 1 or -1. `down_signs`: every entry is 1 or -1.
All inputs are finite; a program needn't handle non-finite values.
Results may differ from a plain program's by a relative error of at most 0.013.
Values may be sent and summed in bfloat16 or wider, within the bound.
No kernel may reach another device: no remote copies, remote signals or barrier semaphores. Data moves between devices by JAX's collectives and lax.ppermute only.
A program may use at most 192 MiB of HBM per device.

v0:
```python
import jax
import jax.numpy as jnp
from jax import lax
from jax.sharding import PartitionSpec as P

D = 8192
QUERY_HEADS = 64
HEAD_SIZE = 128
FF = 16384
NEG = -1e30
EPS = 1e-05


def combine(first, second):
    first_top, first_total, first_out = first
    second_top, second_total, second_out = second
    peak = jnp.maximum(first_top, second_top)
    first_scale = jnp.exp(first_top - peak)
    second_scale = jnp.exp(second_top - peak)
    total = first_total * first_scale + second_total * second_scale
    merged = first_out * first_scale[..., None] + second_out * second_scale[..., None]
    return (peak, total, merged)


def draft_rows(query_rows, group_rows, visible_rows, key_rows, value_rows, factor):
    groups = key_rows.shape[1]
    choose = (group_rows[:, None] == jnp.arange(groups, dtype=jnp.int32)[None, :]).astype(
        jnp.float32
    )
    every_group = (
        jnp.einsum("rd,kgd->rgk", query_rows, key_rows, preferred_element_type=jnp.float32) * factor
    )
    scores = jnp.einsum("rgk,rg->rk", every_group, choose, precision=lax.Precision.HIGHEST)
    masked = jnp.where(visible_rows, scores, NEG)
    peak = jnp.max(masked, axis=-1)
    weights = jnp.where(visible_rows, jnp.exp(masked - peak[:, None]), 0.0)
    total = jnp.sum(weights, axis=-1)
    every_value = jnp.einsum(
        "rk,kgd->rgd", weights.astype(jnp.bfloat16), value_rows, preferred_element_type=jnp.float32
    )
    result = jnp.einsum("rgd,rg->rd", every_value, choose, precision=lax.Precision.HIGHEST)
    return (peak, total, result)


def shards(
    residual,
    queries,
    draft_token_keys,
    draft_token_values,
    cache_keys,
    cached_value_rows,
    tenant_ids,
    tree_mask,
    cache_lengths,
    out_weight,
    out_signs,
    norm_gain,
    gate_weight,
    up_weight,
    down_weight,
    gate_signs,
    up_signs,
    down_signs,
    delta_scale,
):
    tenants = cache_keys.shape[0]
    tokens = tenant_ids.shape[0]
    draft = tokens // tenants
    heads_here = queries.shape[1] // HEAD_SIZE
    groups_here = draft_token_keys.shape[1] // HEAD_SIZE
    group_width = heads_here // groups_here
    ctx_rows = cache_keys.shape[1]
    factor = HEAD_SIZE ** (-0.5)
    sort_order = jnp.argsort(tenant_ids, stable=True)
    inverse = jnp.argsort(sort_order)
    sorted_queries = queries[sort_order]
    query_blocks = sorted_queries.reshape(tenants, draft, groups_here, group_width, HEAD_SIZE)
    draft_key_lines = draft_token_keys[sort_order].reshape(tokens, groups_here, HEAD_SIZE)
    draft_value_lines = draft_token_values[sort_order].reshape(tokens, groups_here, HEAD_SIZE)
    visible = tree_mask[sort_order][:, sort_order] > 0
    first_slot = lax.axis_index("ctx") * ctx_rows
    slot_ids = first_slot + jnp.arange(ctx_rows, dtype=jnp.int32)
    live = (slot_ids[None, :] < cache_lengths[:, None])[:, None, None, None, :]
    cache_key_blocks = cache_keys.reshape(tenants, ctx_rows, groups_here, HEAD_SIZE)
    cache_value_blocks = cached_value_rows.reshape(tenants, ctx_rows, groups_here, HEAD_SIZE)
    scores = (
        jnp.einsum(
            "tqgwd,tjgd->tqgwj", query_blocks, cache_key_blocks, preferred_element_type=jnp.float32
        )
        * factor
    )
    masked = jnp.where(live, scores, NEG)
    peak = jnp.max(masked, axis=-1)
    weights = jnp.where(live, jnp.exp(masked - peak[..., None]), 0.0)
    total = jnp.sum(weights, axis=-1)
    weighted = jnp.einsum(
        "tqgwj,tjgd->tqgwd",
        weights.astype(jnp.bfloat16),
        cache_value_blocks,
        preferred_element_type=jnp.float32,
    )
    part_top = peak.reshape(tokens, heads_here)
    part_total = total.reshape(tokens, heads_here)
    part_out = weighted.reshape(tokens, heads_here, HEAD_SIZE)
    n_ctx = lax.axis_size("ctx")
    all_rows = tokens * heads_here
    share = all_rows // n_ctx
    got_top, got_total, got_out = (
        lax.all_to_all(
            part_top.reshape(1, all_rows), "ctx", split_axis=1, concat_axis=0, tiled=True
        ),
        lax.all_to_all(
            part_total.reshape(1, all_rows), "ctx", split_axis=1, concat_axis=0, tiled=True
        ),
        lax.all_to_all(
            part_out.reshape(1, all_rows, HEAD_SIZE), "ctx", split_axis=1, concat_axis=0, tiled=True
        ),
    )
    summit = jnp.max(got_top, axis=0)
    rescale = jnp.exp(got_top - summit)
    merged = (
        summit,
        jnp.sum(got_total * rescale, axis=0),
        jnp.sum(got_out * rescale[..., None], axis=0),
    )
    first_row = lax.axis_index("ctx") * share
    row_ids = first_row + jnp.arange(share, dtype=jnp.int32)
    token_rows = row_ids // heads_here
    group_rows = row_ids % heads_here // group_width
    query_rows = lax.dynamic_slice_in_dim(
        sorted_queries.reshape(all_rows, HEAD_SIZE), first_row, share, 0
    )
    own = draft_rows(
        query_rows, group_rows, visible[token_rows], draft_key_lines, draft_value_lines, factor
    )
    final_top, final_total, final_out = combine(merged, own)
    finished = (final_out / final_total[:, None]).astype(jnp.bfloat16)
    attention = lax.all_gather(finished, "ctx", axis=0, tiled=True).reshape(
        tokens, heads_here * HEAD_SIZE
    )
    attention_split = attention.reshape(tenants, draft, -1)
    projected = jnp.dot(attention, out_weight, preferred_element_type=jnp.float32)
    out_delta = jnp.einsum(
        "tqh,thf->tqf", attention_split, out_signs, preferred_element_type=jnp.float32
    )
    projected = projected + (
        out_delta * (delta_scale[:, 0] * (QUERY_HEADS * HEAD_SIZE) ** (-0.5))[:, None, None]
    ).reshape(tokens, -1)
    summed_heads = lax.psum(projected.astype(jnp.bfloat16), "kv").astype(jnp.float32)
    hidden = residual[sort_order].astype(jnp.float32) + summed_heads
    squares = lax.psum(jnp.sum(hidden * hidden, axis=1), "ctx")
    normed = (hidden * lax.rsqrt(squares / D + EPS)[:, None] * norm_gain).astype(jnp.bfloat16)
    hidden_units = gate_weight.shape[1]
    piece = lax.all_gather(normed, "ctx", axis=1, tiled=True)
    size = piece.shape[1]
    split_piece = piece.reshape(tenants, draft, size)
    gate_base = jnp.dot(piece, gate_weight, preferred_element_type=jnp.float32)
    up_base = jnp.dot(piece, up_weight, preferred_element_type=jnp.float32)
    gate_delta = jnp.einsum(
        "tqf,tfh->tqh", split_piece, gate_signs, preferred_element_type=jnp.float32
    )
    up_delta = jnp.einsum("tqf,tfh->tqh", split_piece, up_signs, preferred_element_type=jnp.float32)
    gate = gate_base + (gate_delta * (delta_scale[:, 1] * D ** (-0.5))[:, None, None]).reshape(
        tokens, hidden_units
    )
    up_part = up_base + (up_delta * (delta_scale[:, 2] * D ** (-0.5))[:, None, None]).reshape(
        tokens, hidden_units
    )
    active = (jax.nn.silu(gate) * up_part).astype(jnp.bfloat16)
    active_split = active.reshape(tenants, draft, hidden_units)
    down_factor = delta_scale[:, 3] * FF ** (-0.5)
    features_here = residual.shape[1]
    base_part = lax.dot_general(
        down_weight, active, (((0,), (1,)), ((), ())), preferred_element_type=jnp.float32
    )
    delta_part = jnp.einsum(
        "thf,tqh->ftq", down_signs, active_split, preferred_element_type=jnp.float32
    )
    delta_part = delta_part * down_factor[None, :, None]
    lowered = lax.psum_scatter(
        base_part + delta_part.reshape(features_here * lax.axis_size("ctx"), tokens),
        "ctx",
        scatter_dimension=0,
        tiled=True,
    )
    lowered = lax.psum(lowered.astype(jnp.bfloat16), "kv").astype(jnp.float32)
    return (hidden + lowered.T).astype(jnp.bfloat16)[inverse]


def solution(mesh):
    return jax.shard_map(
        shards,
        mesh=mesh,
        in_specs=(
            P(None, "ctx"),
            P(None, "kv"),
            P(None, "kv"),
            P(None, "kv"),
            P(None, "ctx", "kv"),
            P(None, "ctx", "kv"),
            P(),
            P(),
            P(),
            P("kv", "ctx"),
            P(None, "kv", "ctx"),
            P("ctx"),
            P(None, ("kv", "ctx")),
            P(None, ("kv", "ctx")),
            P(("kv", "ctx"), None),
            P(None, None, ("kv", "ctx")),
            P(None, None, ("kv", "ctx")),
            P(None, ("kv", "ctx"), None),
            P(),
        ),
        out_specs=P(None, "ctx"),
        check_vma=False,
    )
```

profile of v0, /device:TPU:0, one launch (start us, length us, event | category | flops | bytes accessed | tf_op | source)
XLA Modules:
  0.0 308.4 jit_solution(11207596414709739598)
XLA Ops:
  6.5 2.8 sort.34
  9.4 0.9 gather_fusion.1
  10.2 0.1 copy.79
  10.4 0.3 reshape.250
  10.7 0.1 broadcast_compare_fusion
  10.7 0.9 bitcast_reduce_fusion
  11.7 1.9 copy-done.3
  13.6 1.3 fusion.3
  14.8 0.1 copy.59
  14.9 0.8 all_to_all.38
  15.7 7.4 %all-to-all-start.2 = ((f32[1,16,128]{2,0,1:T(1,128)}), f32[1,16,128]{2,0,1:T(1,128)S(1)}, u32[]{:S(2)}, u32[]{:S(2)}) async-start(f32[1,16,128]{2,0,1:T(1,128)} %bitcast.17), calls=%async_computation.2 | async-start | bytes 16384 | tf_op jit(solution)/shard_map/all_to_all | solution.py:112
  23.1 1.1 reshape.251
  24.2 3.6 %fusion.9 = f32[2,32,4,8,128]{4,3,1,2,0:T(8,128)S(1)} fusion(f32[2,4,32,8,512]{4,3,2,1,0:T(8,128)} %copy-done.3, f32[2,32,4,8]{3,1,2,0:T(8,128)S(1)} %get-tuple-element.20, pred[2,512]{1,0:T(4,128)(4,1)S(1)} %broadcast_compare_fusion, bf16[2,512,4,128,1]{3,2,1,0,4:T(4,128)(2,1)} %bitcast.112), kind=kOutput, calls=%fused_computation.21 | convolution fusion | flops 273678336 | bytes 6300672 | tf_op jit(solution)/shard_map/tqgwj,tjgd->tqgwd/dot_general | solution.py:96
  27.8 0.1 copy.51
  27.9 0.7 all_to_all.35
  28.7 0.8 all-to-all-done.2
  29.4 5.2 %all-to-all-start.1 = ((f32[1,16,128]{2,0,1:T(1,128)}), f32[1,16,128]{2,0,1:T(1,128)S(1)}, u32[]{:S(2)}, u32[]{:S(2)}) async-start(f32[1,16,128]{2,0,1:T(1,128)} %bitcast.7), calls=%async_computation.1 | async-start | bytes 16384 | tf_op jit(solution)/shard_map/all_to_all | solution.py:109
  34.7 0.2 reshape.253
  35.0 1.1 copy.49
  36.1 5.0 %all-to-all-done.1 = f32[1,16,128]{2,0,1:T(1,128)S(1)} async-done(((f32[1,16,128]{2,0,1:T(1,128)}), f32[1,16,128]{2,0,1:T(1,128)S(1)}, u32[]{:S(2)}, u32[]{:S(2)}) %all-to-all-start.1) | async-done | bytes 8224 | tf_op jit(solution)/shard_map/all_to_all | solution.py:109
  41.1 3.7 %all-to-all-start = ((f32[1,2048,128]{2,0,1:T(1,128)}), f32[1,2048,128]{2,0,1:T(1,128)S(1)}, u32[]{:S(2)}, u32[]{:S(2)}) async-start(f32[1,2048,128]{2,0,1:T(1,128)} %bitcast.5), calls=%async_computation | async-start | bytes 2097152 | tf_op jit(solution)/shard_map/all_to_all | solution.py:115
  44.8 0.1 fusion.30
  45.0 0.7 gather_fusion.5
  45.7 0.6 gather_fusion.2
  46.3 0.1 copy.53
  46.4 0.6 gather_fusion.3
  47.0 0.1 copy.54
  47.2 0.7 gather_fusion.4
  47.8 0.1 copy.56
  47.9 0.7 gather_fusion.6
  48.7 0.2 multiply_reduce_fusion.3
  48.9 0.2 fusion.17
  49.1 0.2 fusion.25
  49.3 0.7 fusion.22
  50.1 17.5 %all-to-all-done = f32[1,2048,128]{2,0,1:T(1,128)S(1)} async-done(((f32[1,2048,128]{2,0,1:T(1,128)}), f32[1,2048,128]{2,0,1:T(1,128)S(1)}, u32[]{:S(2)}, u32[]{:S(2)}) %all-to-all-start) | async-done | bytes 1048608 | tf_op jit(solution)/shard_map/all_to_all | solution.py:115
  67.6 0.3 multiply_reduce_fusion
  68.0 0.1 divide_convert_fusion
  68.1 24.0 %all_gather.6 = bf16[2048,128]{1,0:T(8,128)(2,1)S(1)} all-gather(bf16[128,128]{1,0:T(8,128)(2,1)S(1)} %divide_convert_fusion), channel_id=1, replica_groups=mesh['kv'=2,'ctx'=16] {'ctx'}, dimensions={0}, use_global_device_ids=true | all-gather | bytes 557056 | tf_op jit(solution)/shard_map/all_gather | solution.py:138
  92.1 0.2 reshape_reshape.9
  92.3 0.2 reshape.255
  92.6 5.1 %convolution_multiply_fusion.1 = f32[2,32,512]{2,1,0:T(8,128)S(1)} fusion(bf16[2,32,4096]{2,1,0:T(8,128)(2,1)S(1)} %reshape_reshape.9, bf16[2,4096,512]{2,1,0:T(8,128)(2,1)} %param.29, f32[2]{0:T(128)S(1)} %get-tuple-element.11), kind=kOutput, calls=%fused_computation.22 | convolution fusion | flops 268468224 | bytes 9043976 | tf_op jit(solution)/shard_map/tqh,thf->tqf/dot_general | solution.py:143
  97.6 1.5 fusion.16
  99.2 0.7 gather_fusion
  99.9 17.6 %all-reduce.3.cloned.1.call-done = bf16[64,512]{1,0:T(8,128)(2,1)} async-done(((bf16[64,512]{1,0:T(8,128)(2,1)}), bf16[64,512]{1,0:T(8,128)(2,1)}) %all-reduce.3.cloned.1.call-update) | async-done | bytes 65552 | tf_op jit(solution)/shard_map/psum | solution.py:149
  117.5 1.0 multiply_reduce_fusion.1
  118.5 32.7 %psum.22 = f32[64]{0:T(128)S(1)} all-reduce(f32[64]{0:T(128)S(1)} %multiply_reduce_fusion.1), channel_id=1, replica_groups=mesh['kv'=2,'ctx'=16] {'ctx'}, use_global_device_ids=true, to_apply=%region_10.11 | all-reduce | flops 64 | bytes 512 | tf_op jit(solution)/shard_map/psum | solution.py:151
  151.2 1.6 multiply_convert_fusion
  152.8 0.2 reduce-scatter.2.cloned.1.call-start
  153.0 32.9 %all-gather.2.cloned.1.call-done = bf16[64,8192]{1,0:T(8,128)(2,1)} async-done(((bf16[64,512]{1,0:T(8,128)(2,1)}), bf16[64,8192]{1,0:T(8,128)(2,1)}) %all-gather.2.cloned.1.call-update) | async-done | bytes 1048592 | tf_op jit(solution)/shard_map/all_gather | solution.py:154
  185.9 9.1 %convolution_multiply_fusion.3 = f32[2,32,512]{2,1,0:T(8,128)S(1)} fusion(bf16[2,32,8192]{2,1,0:T(8,128)(2,1)} %bitcast.93, bf16[2,8192,512]{2,1,0:T(8,128)(2,1)} %param.34, f32[2]{0:T(128)S(1)} %get-tuple-element.10), kind=kOutput, calls=%fused_computation.27 | convolution fusion | flops 536903680 | bytes 17956872 | tf_op jit(solution)/shard_map/tqf,tfh->tqh/dot_general | solution.py:159
  195.1 8.8 %convolution_multiply_fusion.2 = f32[2,32,512]{2,1,0:T(8,128)S(1)} fusion(bf16[2,32,8192]{2,1,0:T(8,128)(2,1)S(1)} %bitcast.94, bf16[2,8192,512]{2,1,0:T(8,128)(2,1)} %param.35, f32[2]{0:T(128)S(1)} %get-tuple-element.12), kind=kOutput, calls=%fused_computation.24 | convolution fusion | flops 536903680 | bytes 17956872 | tf_op jit(solution)/shard_map/tqf,tfh->tqh/dot_general | solution.py:162
  204.0 1.6 convolution_add_fusion.2
  205.7 1.6 fusion.15
  207.2 0.2 slice-done.7
  207.5 1.2 slice-done.8
  208.7 1.4 slice-done.9
  210.1 3.0 convolution_multiply_fusion
  213.1 2.9 fusion
  216.1 2.0 sort.35
  218.1 59.5 %reduce-scatter.2.cloned.1.call-done = f32[512,64]{0,1:T(8,128)} async-done(((f32[8192,64]{0,1:T(8,128)}), f32[512,64]{0,1:T(8,128)}) %reduce-scatter.2.cloned.1.call-update) | async-done | bytes 131088 | tf_op jit(solution)/shard_map/reduce_scatter | solution.py:180
  277.7 1.5 convert_bitcast_fusion
  279.3 20.4 %all-reduce.5.cloned.1.call-done = bf16[64,512]{1,0:T(8,128)(2,1)} async-done(((bf16[64,512]{1,0:T(8,128)(2,1)}), bf16[64,512]{1,0:T(8,128)(2,1)}) %all-reduce.5.cloned.1.call-update) | async-done | bytes 65552 | tf_op jit(solution)/shard_map/psum | solution.py:186
  299.7 0.9 add_convert_fusion
  300.6 1.3 gather_fusion.7
  (75 shorter events, 0.7 us)
Async XLA Ops:
  6.5 2.8 copy-start
  6.5 3.8 %copy-start.9 = (bf16[2,512,512]{2,1,0:T(8,128)(2,1)S(1)}, bf16[2,512,512]{2,1,0:T(8,128)(2,1)}, u32[]{:S(2)}) copy-start(bf16[2,512,512]{2,1,0:T(8,128)(2,1)} %param.23) | copy-start | bytes 3145732
  6.5 4.1 %copy-start.14 = (s32[2]{0:T(128)S(1)}, s32[2]{0:T(128)}, u32[]{:S(2)}) copy-start(s32[2]{0:T(128)} %param.27) | copy-start | bytes 28
  10.7 12.3 %copy-start.10 = (bf16[2,512,512]{2,1,0:T(8,128)(2,1)S(1)}, bf16[2,512,512]{2,1,0:T(8,128)(2,1)}, u32[]{:S(2)}) copy-start(bf16[2,512,512]{2,1,0:T(8,128)(2,1)} %param.24) | copy-start | bytes 3145732
  11.6 1.9 copy-start.3
  15.7 13.8 %all-to-all-start.2 = ((f32[1,16,128]{2,0,1:T(1,128)}), f32[1,16,128]{2,0,1:T(1,128)S(1)}, u32[]{:S(2)}, u32[]{:S(2)}) async-start(f32[1,16,128]{2,0,1:T(1,128)} %bitcast.17), calls=%async_computation.2 | async-start | bytes 16384 | tf_op jit(solution)/shard_map/all_to_all | solution.py:112
  27.8 17.2 %copy-start.5 = (bf16[64,512]{1,0:T(8,128)(2,1)S(1)}, bf16[64,512]{1,0:T(8,128)(2,1)}, u32[]{:S(2)}) copy-start(bf16[64,512]{1,0:T(8,128)(2,1)} %param.21) | copy-start | bytes 196612
  27.8 17.9 %copy-start.8 = (s32[64,64]{1,0:T(8,128)S(1)}, s32[64,64]{1,0:T(8,128)}, u32[]{:S(2)}) copy-start(s32[64,64]{1,0:T(8,128)} %param.26) | copy-start | bytes 49156
  27.8 20.1 %copy-start.6 = (bf16[64,512]{1,0:T(8,128)(2,1)S(1)}, bf16[64,512]{1,0:T(8,128)(2,1)}, u32[]{:S(2)}) copy-start(bf16[64,512]{1,0:T(8,128)(2,1)} %param.22) | copy-start | bytes 196612
  27.8 20.8 %copy-start.12 = (f32[2,4]{1,0:T(2,128)S(1)}, f32[2,4]{1,0:T(2,128)}, u32[]{:S(2)}) copy-start(f32[2,4]{1,0:T(2,128)} %param.37) | copy-start | bytes 100
  29.4 11.7 %all-to-all-start.1 = ((f32[1,16,128]{2,0,1:T(1,128)}), f32[1,16,128]{2,0,1:T(1,128)S(1)}, u32[]{:S(2)}, u32[]{:S(2)}) async-start(f32[1,16,128]{2,0,1:T(1,128)} %bitcast.7), calls=%async_computation.1 | async-start | bytes 16384 | tf_op jit(solution)/shard_map/all_to_all | solution.py:109
  41.1 26.5 %all-to-all-start = ((f32[1,2048,128]{2,0,1:T(1,128)}), f32[1,2048,128]{2,0,1:T(1,128)S(1)}, u32[]{:S(2)}, u32[]{:S(2)}) async-start(f32[1,2048,128]{2,0,1:T(1,128)} %bitcast.5), calls=%async_computation | async-start | bytes 2097152 | tf_op jit(solution)/shard_map/all_to_all | solution.py:115
  44.8 72.7 %all-reduce.3.cloned.1.call-start = ((), (), s32[]{:S(2)}) async-start(), calls=%async_computation.4 | async-start | bytes 131072 | tf_op jit(solution)/shard_map/psum | solution.py:149
  92.5 5.1 %copy-start.4 = (bf16[4096,512]{1,0:T(8,128)(2,1)S(1)}, bf16[4096,512]{1,0:T(8,128)(2,1)}, u32[]{:S(2)}) copy-start(bf16[4096,512]{1,0:T(8,128)(2,1)} %param.28) | copy-start | bytes 12582916
  97.6 1.6 copy-start.7
  97.6 53.6 %copy-start.13 = (f32[512]{0:T(512)S(1)}, f32[512]{0:T(512)}, u32[]{:S(2)}) copy-start(f32[512]{0:T(512)} %param.30) | copy-start | bytes 6148
  99.1 86.8 %all-gather.2.cloned.1.call-start = ((), (), s32[]{:S(2)}) async-start(), calls=%async_computation.5 | async-start | bytes 1114112 | tf_op jit(solution)/shard_map/all_gather | solution.py:154
  152.8 124.9 %reduce-scatter.2.cloned.1.call-start = ((), (), s32[]{:S(2)}) async-start(), calls=%async_computation.6 | async-start | bytes 2228224 | tf_op jit(solution)/shard_map/reduce_scatter | solution.py:180
  185.9 9.2 %copy-start.2 = (bf16[64,8192]{1,0:T(8,128)(2,1)S(1)}, bf16[64,8192]{1,0:T(8,128)(2,1)}, u32[]{:S(2)}) copy-start(bf16[64,8192]{1,0:T(8,128)(2,1)} %all-gather.2.cloned.1.call-done) | copy-start | bytes 3145732
  185.9 18.1 %slice-start = ((s8[8388608]{0:T(1024)(128)(4,1)}), s8[4194304]{0:T(1024)(128)(4,1)S(1)}, s32[]{:S(2)}) async-start(s8[8388608]{0:T(1024)(128)(4,1)} %bitcast.95), calls=%async_computation.8 | async-start | bytes 8388608
  185.9 19.7 %slice-start.2 = ((s8[8388608]{0:T(1024)(128)(4,1)}), s8[4194304]{0:T(1024)(128)(4,1)S(1)}, s32[]{:S(2)}) async-start(s8[8388608]{0:T(1024)(128)(4,1)} %bitcast.97), calls=%async_computation.10 | async-start | bytes 8388608
  195.1 8.9 %slice-start.1 = ((s8[8388608]{0:T(1024)(128)(4,1)}), s8[4194304]{0:T(1024)(128)(4,1)S(1)}, s32[]{:S(2)}) async-start(s8[8388608]{0:T(1024)(128)(4,1)} %bitcast.95), calls=%async_computation.9 | async-start | bytes 8388608
  195.1 10.5 %slice-start.3 = ((s8[8388608]{0:T(1024)(128)(4,1)}), s8[4194304]{0:T(1024)(128)(4,1)S(1)}, s32[]{:S(2)}) async-start(s8[8388608]{0:T(1024)(128)(4,1)} %bitcast.97), calls=%async_computation.11 | async-start | bytes 8388608
  204.0 3.2 %slice-start.6 = ((s8[16777216]{0:T(1024)(128)(4,1)}), s8[4194304]{0:T(1024)(128)(4,1)S(1)}, s32[]{:S(2)}) async-start(s8[16777216]{0:T(1024)(128)(4,1)} %bitcast.102), calls=%async_computation.14 | async-start | bytes 8388608
  204.0 3.5 %slice-start.7 = ((s8[16777216]{0:T(1024)(128)(4,1)}), s8[4194304]{0:T(1024)(128)(4,1)S(1)}, s32[]{:S(2)}) async-start(s8[16777216]{0:T(1024)(128)(4,1)} %bitcast.102), calls=%async_computation.15 | async-start | bytes 8388608
  204.0 4.6 %slice-start.8 = ((s8[16777216]{0:T(1024)(128)(4,1)}), s8[4194304]{0:T(1024)(128)(4,1)S(1)}, s32[]{:S(2)}) async-start(s8[16777216]{0:T(1024)(128)(4,1)} %bitcast.102), calls=%async_computation.16 | async-start | bytes 8388608
  205.6 4.4 %slice-start.9 = ((s8[16777216]{0:T(1024)(128)(4,1)}), s8[4194304]{0:T(1024)(128)(4,1)S(1)}, s32[]{:S(2)}) async-start(s8[16777216]{0:T(1024)(128)(4,1)} %bitcast.102), calls=%async_computation.17 | async-start | bytes 8388608
  205.6 7.4 %slice-start.4 = ((s8[8388608]{0:T(1024)(128)(4,1)}), s8[4194304]{0:T(1024)(128)(4,1)S(1)}, s32[]{:S(2)}) async-start(s8[8388608]{0:T(1024)(128)(4,1)} %bitcast.99), calls=%async_computation.12 | async-start | bytes 8388608
  210.1 3.0 slice-start.5
  213.1 86.6 %copy-start.11 = (bf16[64,512]{1,0:T(8,128)(2,1)S(1)}, bf16[64,512]{1,0:T(8,128)(2,1)}, u32[]{:S(2)}) copy-start(bf16[64,512]{1,0:T(8,128)(2,1)} %all-reduce.3.cloned.1.call-done) | copy-start | bytes 196612
  213.1 88.8 %copy-start.1 = (bf16[64,4096]{1,0:T(8,128)(2,1)S(1)}, bf16[64,4096]{1,0:T(8,128)(2,1)}, u32[]{:S(2)}) copy-start(bf16[64,4096]{1,0:T(8,128)(2,1)} %param.20) | copy-start | bytes 1572868
  216.1 83.7 %all-reduce.5.cloned.1.call-start = ((), (), s32[]{:S(2)}) async-start(), calls=%async_computation.7 | async-start | bytes 131072 | tf_op jit(solution)/shard_map/psum | solution.py:186
Sparse Core Ops, SparseCore 0:
  99.3 18.2 all-reduce.2
  152.9 32.9 all-gather.1
  216.2 61.4 reduce-scatter.1
  279.8 19.8 all-reduce.4
where the time goes:
time: 309 us; the launch traced here: 308 us
  waiting for transfers between devices  154 us (50%)
  blocking collectives  56.7 us (18%)
  matrix products  39 us (13%)
  starting transfers between devices  16.6 us (5%)
  local copies, waits for them, and re-layouts  16.5 us (5%)
  between operations  13.7 us (4%)
  other arithmetic  12.1 us (4%)
    reduce_scatter x1, waiting for transfers between devices, shards(): lax.psum_scatter(base_part + delta_part.reshape(features_here * lax.axis_...  59.5 us
    all_gather x1, waiting for transfers between devices, shards(): piece = lax.all_gather(normed, 'ctx', axis=1, tiled=True)  32.9 us
    psum x1, blocking collectives, shards(): squares = lax.psum(jnp.sum(hidden * hidden, axis=1), 'ctx')  32.7 us
    all_gather x1, blocking collectives, shards(): lax.all_gather(finished, 'ctx', axis=0, tiled=True)  24 us
    psum x1, waiting for transfers between devices, shards(): lowered = lax.psum(lowered.astype(jnp.bfloat16), 'kv').astype(jnp.float32)  20.4 us
    psum x1, waiting for transfers between devices, shards(): lax.psum(projected.astype(jnp.bfloat16), 'kv').astype(jnp.float32)  17.6 us
    all_to_all x1, waiting for transfers between devices, shards(): lax.all_to_all(part_out.reshape(1, all_rows, HEAD_SIZE), 'ctx', split_axi...  17.5 us
    dot_general x1, matrix products, shards(): jnp.einsum('tqf,tfh->tqh', split_piece, gate_signs, preferred_element_typ...  9.14 us
  transfers between devices with their start and end apart: 7, of which 7 were waited for; matrix products, arithmetic and copies ran while one was open for 5% of the time, Pallas kernels for 0%

commit v1 on v0

--- a/solution.py
+++ b/solution.py
@@ -151,7 +151,7 @@
     squares = lax.psum(jnp.sum(hidden * hidden, axis=1), "ctx")
     normed = (hidden * lax.rsqrt(squares / D + EPS)[:, None] * norm_gain).astype(jnp.bfloat16)
     hidden_units = gate_weight.shape[1]
-    piece = lax.all_gather(normed, "ctx", axis=1, tiled=True)
+    piece = jnp.concatenate(lax.all_gather(normed, "ctx"), axis=1)
     size = piece.shape[1]
     split_piece = piece.reshape(tenants, draft, size)
     gate_base = jnp.dot(piece, gate_weight, preferred_element_type=jnp.float32)

time: 309 us -> 314 us (1.016)
  local copies, waits for them, and re-layouts: 16.5 us -> 21.1 us
  transfers between devices with their start and end apart: 7 -> 7, of which waited for: 7 -> 7; matrix products, arithmetic and copies ran while one was open for 5% -> 4% of each run, Pallas kernels for 0% -> 0%
where the time goes in v1:
time: 314 us; the launch traced here: 313 us
  waiting for transfers between devices  154 us (49%)
  blocking collectives  56.7 us (18%)
  matrix products  38.7 us (12%)
  local copies, waits for them, and re-layouts  21.1 us (7%)
  starting transfers between devices  16.6 us (5%)
  between operations  13.7 us (4%)
  other arithmetic  12.1 us (4%)
    reduce_scatter x1, waiting for transfers between devices, shards(): lax.psum_scatter(base_part + delta_part.reshape(features_here * lax.axis_...  58.9 us
    all_gather x1, waiting for transfers between devices, shards(): piece = jnp.concatenate(lax.all_gather(normed, 'ctx'), axis=1)  34.1 us
    psum x1, blocking collectives, shards(): squares = lax.psum(jnp.sum(hidden * hidden, axis=1), 'ctx')  32.7 us
    all_gather x1, blocking collectives, shards(): lax.all_gather(finished, 'ctx', axis=0, tiled=True)  24 us
    psum x1, waiting for transfers between devices, shards(): lowered = lax.psum(lowered.astype(jnp.bfloat16), 'kv').astype(jnp.float32)  20.4 us
    psum x1, waiting for transfers between devices, shards(): lax.psum(projected.astype(jnp.bfloat16), 'kv').astype(jnp.float32)  17.6 us
    all_to_all x1, waiting for transfers between devices, shards(): lax.all_to_all(part_out.reshape(1, all_rows, HEAD_SIZE), 'ctx', split_axi...  17.5 us
    dot_general x1, matrix products, shards(): jnp.einsum('tqf,tfh->tqh', split_piece, gate_signs, preferred_element_typ...  8.82 us
  transfers between devices with their start and end apart: 7, of which 7 were waited for; matrix products, arithmetic and copies ran while one was open for 4% of the time, Pallas kernels for 0%

profile of v1, /device:TPU:0, one launch (start us, length us, event | category | flops | bytes accessed | tf_op | source)
XLA Modules:
  0.0 313.3 jit_solution(4109980580644726731)
XLA Ops:
  6.5 2.8 sort.34
  9.4 0.9 gather_fusion.1
  10.2 0.1 copy.83
  10.4 0.3 reshape.253
  10.7 0.9 bitcast_reduce_fusion
  11.7 1.9 copy-done.2
  13.6 1.3 fusion.3
  14.8 0.1 copy.62
  14.9 0.8 all_to_all.38
  15.7 7.4 %all-to-all-start.2 = ((f32[1,16,128]{2,0,1:T(1,128)}), f32[1,16,128]{2,0,1:T(1,128)S(1)}, u32[]{:S(2)}, u32[]{:S(2)}) async-start(f32[1,16,128]{2,0,1:T(1,128)} %bitcast.17), calls=%async_computation.2 | async-start | bytes 16384 | tf_op jit(solution)/shard_map/all_to_all | solution.py:112
  23.1 1.1 reshape.254
  24.2 3.6 %fusion.9 = f32[2,32,4,8,128]{4,3,1,2,0:T(8,128)S(1)} fusion(f32[2,4,32,8,512]{4,3,2,1,0:T(8,128)} %copy-done.2, f32[2,32,4,8]{3,1,2,0:T(8,128)S(1)} %get-tuple-element.20, pred[2,512]{1,0:T(4,128)(4,1)S(1)} %broadcast_compare_fusion, bf16[2,512,4,128,1]{3,2,1,0,4:T(4,128)(2,1)} %bitcast.122), kind=kOutput, calls=%fused_computation.21 | convolution fusion | flops 273678336 | bytes 6300672 | tf_op jit(solution)/shard_map/tqgwj,tjgd->tqgwd/dot_general | solution.py:96
  27.8 0.1 copy.54
  27.9 0.7 all_to_all.35
  28.7 0.8 all-to-all-done.2
  29.4 5.2 %all-to-all-start.1 = ((f32[1,16,128]{2,0,1:T(1,128)}), f32[1,16,128]{2,0,1:T(1,128)S(1)}, u32[]{:S(2)}, u32[]{:S(2)}) async-start(f32[1,16,128]{2,0,1:T(1,128)} %bitcast.7), calls=%async_computation.1 | async-start | bytes 16384 | tf_op jit(solution)/shard_map/all_to_all | solution.py:109
  34.7 0.2 reshape.256
  35.0 1.1 copy.52
  36.1 5.0 %all-to-all-done.1 = f32[1,16,128]{2,0,1:T(1,128)S(1)} async-done(((f32[1,16,128]{2,0,1:T(1,128)}), f32[1,16,128]{2,0,1:T(1,128)S(1)}, u32[]{:S(2)}, u32[]{:S(2)}) %all-to-all-start.1) | async-done | bytes 8224 | tf_op jit(solution)/shard_map/all_to_all | solution.py:109
  41.1 3.7 %all-to-all-start = ((f32[1,2048,128]{2,0,1:T(1,128)}), f32[1,2048,128]{2,0,1:T(1,128)S(1)}, u32[]{:S(2)}, u32[]{:S(2)}) async-start(f32[1,2048,128]{2,0,1:T(1,128)} %bitcast.5), calls=%async_computation | async-start | bytes 2097152 | tf_op jit(solution)/shard_map/all_to_all | solution.py:115
  45.0 0.7 gather_fusion.5
  45.7 0.6 gather_fusion.2
  46.4 0.6 gather_fusion.3
  47.0 0.1 copy.57
  47.2 0.7 gather_fusion.4
  47.8 0.1 copy.59
  47.9 0.7 gather_fusion.6
  48.7 0.2 multiply_reduce_fusion.3
  48.9 0.2 fusion.17
  49.1 0.2 fusion.25
  49.3 0.7 fusion.22
  50.1 17.5 %all-to-all-done = f32[1,2048,128]{2,0,1:T(1,128)S(1)} async-done(((f32[1,2048,128]{2,0,1:T(1,128)}), f32[1,2048,128]{2,0,1:T(1,128)S(1)}, u32[]{:S(2)}, u32[]{:S(2)}) %all-to-all-start) | async-done | bytes 1048608 | tf_op jit(solution)/shard_map/all_to_all | solution.py:115
  67.6 0.3 multiply_reduce_fusion
  68.0 0.1 divide_convert_fusion
  68.1 24.0 %all_gather.9 = bf16[2048,128]{1,0:T(8,128)(2,1)S(1)} all-gather(bf16[128,128]{1,0:T(8,128)(2,1)S(1)} %divide_convert_fusion), channel_id=1, replica_groups=mesh['kv'=2,'ctx'=16] {'ctx'}, dimensions={0}, use_global_device_ids=true | all-gather | bytes 557056 | tf_op jit(solution)/shard_map/all_gather | solution.py:138
  92.1 0.2 reshape_reshape.12
  92.3 0.2 reshape.258
  92.6 5.1 %convolution_multiply_fusion.1 = f32[2,32,512]{2,1,0:T(8,128)S(1)} fusion(bf16[2,32,4096]{2,1,0:T(8,128)(2,1)S(1)} %reshape_reshape.12, bf16[2,4096,512]{2,1,0:T(8,128)(2,1)} %param.29, f32[2]{0:T(128)S(1)} %get-tuple-element.11), kind=kOutput, calls=%fused_computation.22 | convolution fusion | flops 268468224 | bytes 9043976 | tf_op jit(solution)/shard_map/tqh,thf->tqf/dot_general | solution.py:143
  97.6 1.5 fusion.16
  99.2 0.7 gather_fusion
  99.9 17.6 %all-reduce.3.cloned.1.call-done = bf16[64,512]{1,0:T(8,128)(2,1)} async-done(((bf16[64,512]{1,0:T(8,128)(2,1)}), bf16[64,512]{1,0:T(8,128)(2,1)}) %all-reduce.3.cloned.1.call-update) | async-done | bytes 65552 | tf_op jit(solution)/shard_map/psum | solution.py:149
  117.5 1.0 multiply_reduce_fusion.1
  118.5 32.7 %psum.22 = f32[64]{0:T(128)S(1)} all-reduce(f32[64]{0:T(128)S(1)} %multiply_reduce_fusion.1), channel_id=1, replica_groups=mesh['kv'=2,'ctx'=16] {'ctx'}, use_global_device_ids=true, to_apply=%region_10.11 | all-reduce | flops 64 | bytes 512 | tf_op jit(solution)/shard_map/psum | solution.py:151
  151.2 1.6 multiply_convert_fusion
  152.8 0.2 reduce-scatter.2.cloned.1.call-start
  153.0 34.1 %all-gather.3.cloned.1.call-done = bf16[1024,512]{1,0:T(8,128)(2,1)} async-done(((bf16[64,512]{1,0:T(8,128)(2,1)}), bf16[1024,512]{1,0:T(8,128)(2,1)}) %all-gather.3.cloned.1.call-update) | async-done | bytes 1048592 | tf_op jit(solution)/shard_map/all_gather | solution.py:154
  187.1 2.9 copy.109
  190.0 1.6 reshape_reshape.13
  191.6 0.1 copy.84
  191.7 8.8 %convolution_multiply_fusion.3 = f32[2,32,512]{2,1,0:T(8,128)S(1)} fusion(bf16[2,32,8192]{2,1,0:T(8,128)(2,1)S(1)} %reshape_reshape.13, bf16[2,8192,512]{2,1,0:T(8,128)(2,1)} %param.34, f32[2]{0:T(128)S(1)} %get-tuple-element.10), kind=kOutput, calls=%fused_computation.27 | convolution fusion | flops 536903680 | bytes 17956872 | tf_op jit(solution)/shard_map/tqf,tfh->tqh/dot_general | solution.py:159
  200.6 8.8 %convolution_multiply_fusion.2 = f32[2,32,512]{2,1,0:T(8,128)S(1)} fusion(bf16[2,32,8192]{2,1,0:T(8,128)(2,1)S(1)} %reshape_reshape.13, bf16[2,8192,512]{2,1,0:T(8,128)(2,1)} %param.35, f32[2]{0:T(128)S(1)} %get-tuple-element.12), kind=kOutput, calls=%fused_computation.24 | convolution fusion | flops 536903680 | bytes 17956872 | tf_op jit(solution)/shard_map/tqf,tfh->tqh/dot_general | solution.py:162
  209.5 1.6 convolution_add_fusion.2
  211.1 1.6 fusion.15
  212.7 0.2 slice-done.7
  212.9 1.2 slice-done.8
  214.1 1.4 slice-done.9
  215.5 3.0 convolution_multiply_fusion
  218.6 2.9 fusion
  221.6 2.0 sort.35
  223.6 58.9 %reduce-scatter.2.cloned.1.call-done = f32[512,64]{0,1:T(8,128)} async-done(((f32[8192,64]{0,1:T(8,128)}), f32[512,64]{0,1:T(8,128)}) %reduce-scatter.2.cloned.1.call-update) | async-done | bytes 131088 | tf_op jit(solution)/shard_map/reduce_scatter | solution.py:180
  282.5 1.5 convert_bitcast_fusion
  284.1 20.4 %all-reduce.5.cloned.1.call-done = bf16[64,512]{1,0:T(8,128)(2,1)} async-done(((bf16[64,512]{1,0:T(8,128)(2,1)}), bf16[64,512]{1,0:T(8,128)(2,1)}) %all-reduce.5.cloned.1.call-update) | async-done | bytes 65552 | tf_op jit(solution)/shard_map/psum | solution.py:186
  304.5 0.9 add_convert_fusion
  305.4 1.3 gather_fusion.7
  (78 shorter events, 0.9 us)
Async XLA Ops:
  6.5 2.8 copy-start
  6.5 3.8 %copy-start.9 = (bf16[2,512,512]{2,1,0:T(8,128)(2,1)S(1)}, bf16[2,512,512]{2,1,0:T(8,128)(2,1)}, u32[]{:S(2)}) copy-start(bf16[2,512,512]{2,1,0:T(8,128)(2,1)} %param.23) | copy-start | bytes 3145732
  6.5 4.1 %copy-start.14 = (s32[2]{0:T(128)S(1)}, s32[2]{0:T(128)}, u32[]{:S(2)}) copy-start(s32[2]{0:T(128)} %param.27) | copy-start | bytes 28
  10.7 12.3 %copy-start.10 = (bf16[2,512,512]{2,1,0:T(8,128)(2,1)S(1)}, bf16[2,512,512]{2,1,0:T(8,128)(2,1)}, u32[]{:S(2)}) copy-start(bf16[2,512,512]{2,1,0:T(8,128)(2,1)} %param.24) | copy-start | bytes 3145732
  11.6 1.9 copy-start.2
  15.7 13.8 %all-to-all-start.2 = ((f32[1,16,128]{2,0,1:T(1,128)}), f32[1,16,128]{2,0,1:T(1,128)S(1)}, u32[]{:S(2)}, u32[]{:S(2)}) async-start(f32[1,16,128]{2,0,1:T(1,128)} %bitcast.17), calls=%async_computation.2 | async-start | bytes 16384 | tf_op jit(solution)/shard_map/all_to_all | solution.py:112
  27.8 17.2 %copy-start.5 = (bf16[64,512]{1,0:T(8,128)(2,1)S(1)}, bf16[64,512]{1,0:T(8,128)(2,1)}, u32[]{:S(2)}) copy-start(bf16[64,512]{1,0:T(8,128)(2,1)} %param.21) | copy-start | bytes 196612
  27.8 17.9 %copy-start.8 = (s32[64,64]{1,0:T(8,128)S(1)}, s32[64,64]{1,0:T(8,128)}, u32[]{:S(2)}) copy-start(s32[64,64]{1,0:T(8,128)} %param.26) | copy-start | bytes 49156
  27.8 20.1 %copy-start.6 = (bf16[64,512]{1,0:T(8,128)(2,1)S(1)}, bf16[64,512]{1,0:T(8,128)(2,1)}, u32[]{:S(2)}) copy-start(bf16[64,512]{1,0:T(8,128)(2,1)} %param.22) | copy-start | bytes 196612
  27.8 20.8 %copy-start.12 = (f32[2,4]{1,0:T(2,128)S(1)}, f32[2,4]{1,0:T(2,128)}, u32[]{:S(2)}) copy-start(f32[2,4]{1,0:T(2,128)} %param.37) | copy-start | bytes 100
  29.4 11.7 %all-to-all-start.1 = ((f32[1,16,128]{2,0,1:T(1,128)}), f32[1,16,128]{2,0,1:T(1,128)S(1)}, u32[]{:S(2)}, u32[]{:S(2)}) async-start(f32[1,16,128]{2,0,1:T(1,128)} %bitcast.7), calls=%async_computation.1 | async-start | bytes 16384 | tf_op jit(solution)/shard_map/all_to_all | solution.py:109
  41.1 26.5 %all-to-all-start = ((f32[1,2048,128]{2,0,1:T(1,128)}), f32[1,2048,128]{2,0,1:T(1,128)S(1)}, u32[]{:S(2)}, u32[]{:S(2)}) async-start(f32[1,2048,128]{2,0,1:T(1,128)} %bitcast.5), calls=%async_computation | async-start | bytes 2097152 | tf_op jit(solution)/shard_map/all_to_all | solution.py:115
  44.8 72.7 %all-reduce.3.cloned.1.call-start = ((), (), s32[]{:S(2)}) async-start(), calls=%async_computation.4 | async-start | bytes 131072 | tf_op jit(solution)/shard_map/psum | solution.py:149
  92.5 5.1 %copy-start.3 = (bf16[4096,512]{1,0:T(8,128)(2,1)S(1)}, bf16[4096,512]{1,0:T(8,128)(2,1)}, u32[]{:S(2)}) copy-start(bf16[4096,512]{1,0:T(8,128)(2,1)} %param.28) | copy-start | bytes 12582916
  97.6 1.6 copy-start.7
  97.6 53.6 %copy-start.13 = (f32[512]{0:T(512)S(1)}, f32[512]{0:T(512)}, u32[]{:S(2)}) copy-start(f32[512]{0:T(512)} %param.30) | copy-start | bytes 6148
  99.1 87.9 %all-gather.3.cloned.1.call-start = ((), (), s32[]{:S(2)}) async-start(), calls=%async_computation.7 | async-start | bytes 1114112 | tf_op jit(solution)/shard_map/all_gather | solution.py:154
  152.8 129.8 %reduce-scatter.2.cloned.1.call-start = ((), (), s32[]{:S(2)}) async-start(), calls=%async_computation.5 | async-start | bytes 2228224 | tf_op jit(solution)/shard_map/reduce_scatter | solution.py:180
  187.1 4.5 %copy-start.4 = (bf16[1024,512]{1,0:T(8,128)(2,1)S(1)}, bf16[1024,512]{1,0:T(8,128)(2,1)}, u32[]{:S(2)}) copy-start(bf16[1024,512]{1,0:T(8,128)(2,1)} %all-gather.3.cloned.1.call-done) | copy-start | bytes 3145732
  191.7 17.8 %slice-start = ((s8[8388608]{0:T(1024)(128)(4,1)}), s8[4194304]{0:T(1024)(128)(4,1)S(1)}, s32[]{:S(2)}) async-start(s8[8388608]{0:T(1024)(128)(4,1)} %bitcast.100), calls=%async_computation.8 | async-start | bytes 8388608
  191.7 19.4 %slice-start.2 = ((s8[8388608]{0:T(1024)(128)(4,1)}), s8[4194304]{0:T(1024)(128)(4,1)S(1)}, s32[]{:S(2)}) async-start(s8[8388608]{0:T(1024)(128)(4,1)} %bitcast.102), calls=%async_computation.10 | async-start | bytes 8388608
  200.5 8.9 %slice-start.1 = ((s8[8388608]{0:T(1024)(128)(4,1)}), s8[4194304]{0:T(1024)(128)(4,1)S(1)}, s32[]{:S(2)}) async-start(s8[8388608]{0:T(1024)(128)(4,1)} %bitcast.100), calls=%async_computation.9 | async-start | bytes 8388608
  200.6 10.5 %slice-start.3 = ((s8[8388608]{0:T(1024)(128)(4,1)}), s8[4194304]{0:T(1024)(128)(4,1)S(1)}, s32[]{:S(2)}) async-start(s8[8388608]{0:T(1024)(128)(4,1)} %bitcast.102), calls=%async_computation.11 | async-start | bytes 8388608
  209.5 3.2 %slice-start.6 = ((s8[16777216]{0:T(1024)(128)(4,1)}), s8[4194304]{0:T(1024)(128)(4,1)S(1)}, s32[]{:S(2)}) async-start(s8[16777216]{0:T(1024)(128)(4,1)} %bitcast.109), calls=%async_computation.14 | async-start | bytes 8388608
  209.5 3.5 %slice-start.7 = ((s8[16777216]{0:T(1024)(128)(4,1)}), s8[4194304]{0:T(1024)(128)(4,1)S(1)}, s32[]{:S(2)}) async-start(s8[16777216]{0:T(1024)(128)(4,1)} %bitcast.109), calls=%async_computation.15 | async-start | bytes 8388608
  209.5 4.6 %slice-start.8 = ((s8[16777216]{0:T(1024)(128)(4,1)}), s8[4194304]{0:T(1024)(128)(4,1)S(1)}, s32[]{:S(2)}) async-start(s8[16777216]{0:T(1024)(128)(4,1)} %bitcast.109), calls=%async_computation.16 | async-start | bytes 8388608
  211.1 4.4 %slice-start.9 = ((s8[16777216]{0:T(1024)(128)(4,1)}), s8[4194304]{0:T(1024)(128)(4,1)S(1)}, s32[]{:S(2)}) async-start(s8[16777216]{0:T(1024)(128)(4,1)} %bitcast.109), calls=%async_computation.17 | async-start | bytes 8388608
  211.1 7.4 %slice-start.4 = ((s8[8388608]{0:T(1024)(128)(4,1)}), s8[4194304]{0:T(1024)(128)(4,1)S(1)}, s32[]{:S(2)}) async-start(s8[8388608]{0:T(1024)(128)(4,1)} %bitcast.106), calls=%async_computation.12 | async-start | bytes 8388608
  215.5 3.0 slice-start.5
  218.6 86.0 %copy-start.11 = (bf16[64,512]{1,0:T(8,128)(2,1)S(1)}, bf16[64,512]{1,0:T(8,128)(2,1)}, u32[]{:S(2)}) copy-start(bf16[64,512]{1,0:T(8,128)(2,1)} %all-reduce.3.cloned.1.call-done) | copy-start | bytes 196612
  218.6 88.2 %copy-start.1 = (bf16[64,4096]{1,0:T(8,128)(2,1)S(1)}, bf16[64,4096]{1,0:T(8,128)(2,1)}, u32[]{:S(2)}) copy-start(bf16[64,4096]{1,0:T(8,128)(2,1)} %param.20) | copy-start | bytes 1572868
  221.5 83.0 %all-reduce.5.cloned.1.call-start = ((), (), s32[]{:S(2)}) async-start(), calls=%async_computation.6 | async-start | bytes 131072 | tf_op jit(solution)/shard_map/psum | solution.py:186
Sparse Core Ops, SparseCore 0:
  99.3 18.2 all-reduce.2
  152.9 34.1 all-gather.2
  221.6 60.8 reduce-scatter.1
  284.6 19.8 all-reduce.4
